TPU v7x, 1024 devices: a whole 4x8x16 slice. The times are simulated.
1024 devices in a mesh: kv: 8 (over y), key: 16 (over z), tok: 8 (over x, core).
Axes of the slice: x: 4, y: 8, z: 16, core: 2. Of those that a mesh axis runs over, the one named last changes fastest.
Arguments:
- queries: bfloat16 [4096, 8192], P('key', ('kv', 'tok')), may hold values from -200 to 200
- keys: bfloat16 [4096, 1024], P('key', 'kv'), may hold values from -8 to 8
- values: bfloat16 [4096, 1024], P('key', 'kv'), may hold values from -6 to 6
- doc_ids: int32 [4096], replicated, may hold values from 0 to 5, never falling along the last dimension, each value on 1 to 2048 neighbouring positions
- out_weight: bfloat16 [8192, 8192], P('kv', 'tok'), may hold values from -0.0625 to 0.0625
Outputs:
- mixed: bfloat16 [4096, 8192], P(('key', 'kv'), 'tok')
Inputs may be any that keep to these rules, and one draw needn't show every extreme that they name: `doc_ids`: document numbers never fall along the window; a document covers at most 2048 positions and some document covers exactly that many.
All inputs are finite; a program needn't handle non-finite values.
Results may differ from a plain program's by a relative error of at most 0.014.
Values may be sent and summed in bfloat16 or wider, within the bound.
No kernel may reach another device: no remote copies, remote signals or barrier semaphores. Data moves between devices by JAX's collectives and lax.ppermute only.
A program may use at most 32 MiB of HBM per device.

v0:
```python
import math

import jax
import jax.numpy as jnp
from jax import lax
from jax.experimental import pallas as pl
from jax.experimental.pallas import tpu as pltpu
from jax.sharding import PartitionSpec as P


HEAD_SIZE = 128
REACH = 8
LOW = -1e30
MOST_DOC = 5
LANES = 128
CORES = 2
PAIR = 2
NEEDED = REACH // PAIR
FACTOR = math.log2(math.e) / math.sqrt(HEAD_SIZE)

VMEM = pl.BlockSpec(memory_space=pltpu.VMEM)
SMEM = pl.BlockSpec(memory_space=pltpu.SMEM)


def dot(a, b, contract):
    return lax.dot_general(a, b, (contract, ((), ())), preferred_element_type=jnp.float32)


def first_kernel(index_ref, docs_ref, first_ref):
    query_count = first_ref.shape[1]
    docs = docs_ref[...]
    place = lax.broadcasted_iota(jnp.int32, (1, query_count), 1) + index_ref[0] * query_count
    place = place.astype(jnp.float32)
    first = jnp.zeros((1, query_count), jnp.float32)
    for number in range(1, MOST_DOC + 1):
        smaller = jnp.where(docs < number, 1.0, 0.0)
        begins = jnp.sum(jnp.sum(smaller, axis=0, keepdims=True), axis=1, keepdims=True)
        first = jnp.where(begins <= place, jnp.maximum(first, begins), first)
    first_ref[...] = first


def find_first(index, docs, query_count):
    return pl.pallas_call(
        first_kernel,
        out_shape=jax.ShapeDtypeStruct((1, query_count), jnp.float32),
        in_specs=[SMEM, VMEM],
        out_specs=VMEM,
        compiler_params=pltpu.CompilerParams(vmem_limit_bytes=4 << 20),
        name="first",
    )(index, docs)


def earliest(own, source_parity, taker_parity):
    return own // PAIR - NEEDED + taker_parity * (1 - source_parity)


def pick_kernel(index_ref, ranges_ref, out_ref):
    own = index_ref[0]
    count = ranges_ref.shape[0]
    takers = out_ref.shape[0] // PAIR
    for parity in range(PAIR):
        begin = earliest(own, lax.rem(own, PAIR), parity)
        for place in range(NEEDED):
            block = ranges_ref[lax.rem(begin + place + count, count)]
            for taker in range(takers):
                out_ref[parity * takers + taker, place] = block


def pick(index, ranges, taker_count):
    return pl.pallas_call(
        pick_kernel,
        out_shape=jax.ShapeDtypeStruct((taker_count, NEEDED) + ranges.shape[1:], jnp.bfloat16),
        in_specs=[SMEM, VMEM],
        out_specs=VMEM,
        compiler_params=pltpu.CompilerParams(vmem_limit_bytes=8 << 20),
        name="pick",
    )(index, ranges)


def mask_half(scores, own, core, first, blocks_shape, query_count):
    source_count, place_count, rows, _ = blocks_shape
    row = lax.broadcasted_iota(jnp.int32, (rows, query_count), 0).astype(jnp.float32)
    chips = source_count // PAIR
    pieces = []
    for source in range(source_count):
        parity, chip = source // chips, source % chips
        begin = earliest(own, parity, lax.rem(own, PAIR))
        for place in range(place_count):
            number = (begin + place) * PAIR + parity
            start = number * query_count + (chip * CORES + core) * rows
            at = (source * place_count + place) * rows
            allowed = row >= first - start.astype(jnp.float32)
            pieces.append(jnp.where(allowed, scores[at : at + rows] * FACTOR, LOW))
    return pieces


def near_kernel(
    index_ref, first_ref, queries_ref, keys_ref, values_ref, blocks_ref, stats_ref, sums_ref
):
    own, core = index_ref[0], lax.rem(index_ref[1], CORES)
    query_count = queries_ref.shape[0]
    first = first_ref[...]
    blocks = blocks_ref[...].reshape(-1, 2 * HEAD_SIZE)
    queries = queries_ref[...]
    scores = dot(blocks[:, :HEAD_SIZE], queries, ((1,), (1,)))
    pieces = mask_half(scores, own, core, first, blocks_ref.shape, query_count)
    scores = dot(keys_ref[...], queries, ((1,), (1,)))
    row = lax.broadcasted_iota(jnp.int32, scores.shape, 0)
    lane = lax.broadcasted_iota(jnp.int32, scores.shape, 1)
    begin = first - (own * query_count).astype(jnp.float32)
    allowed = (row <= lane) & (row.astype(jnp.float32) >= begin)
    pieces.append(jnp.where(allowed, scores * FACTOR, LOW))
    scores = jnp.concatenate(pieces, axis=0)
    highest = jnp.max(scores, axis=0, keepdims=True)
    weights = jnp.exp2(scores - highest)
    stats_ref[0:1, :] = highest
    stats_ref[1:2, :] = jnp.sum(weights, axis=0, keepdims=True)
    values = jnp.concatenate([blocks[:, HEAD_SIZE:], values_ref[...]], axis=0)
    sums_ref[...] = dot(values, weights.astype(jnp.bfloat16), ((0,), (0,)))


def far_kernel(index_ref, first_ref, queries_ref, blocks_ref, stats_ref, sums_ref, out_ref):
    own, core = index_ref[0], lax.rem(index_ref[1], CORES)
    query_count = queries_ref.shape[0]
    blocks = blocks_ref[...].reshape(-1, 2 * HEAD_SIZE)
    scores = dot(blocks[:, :HEAD_SIZE], queries_ref[...], ((1,), (1,)))
    pieces = mask_half(scores, own, 1 - core, first_ref[...], blocks_ref.shape, query_count)
    scores = jnp.concatenate(pieces, axis=0)
    before = stats_ref[0:1, :]
    highest = jnp.maximum(before, jnp.max(scores, axis=0, keepdims=True))
    weights = jnp.exp2(scores - highest)
    keep = jnp.exp2(before - highest)
    total = keep * stats_ref[1:2, :] + jnp.sum(weights, axis=0, keepdims=True)
    weighted = dot(blocks[:, HEAD_SIZE:], weights.astype(jnp.bfloat16), ((0,), (0,)))
    attn = ((keep * sums_ref[...] + weighted) * (1.0 / total)).astype(jnp.bfloat16)
    for target in range(out_ref.shape[0]):
        out_ref[target] = attn


def cost(queries, key_count):
    scores = queries.shape[0] * key_count
    return pl.CostEstimate(
        flops=4 * HEAD_SIZE * scores, transcendentals=scores, bytes_accessed=1 << 20
    )


def attend_near(index, first, queries, keys, values, blocks):
    query_count = queries.shape[0]
    return pl.pallas_call(
        near_kernel,
        out_shape=[
            jax.ShapeDtypeStruct((8, query_count), jnp.float32),
            jax.ShapeDtypeStruct((HEAD_SIZE, query_count), jnp.float32),
        ],
        in_specs=[SMEM] + [VMEM] * 5,
        out_specs=[VMEM, VMEM],
        compiler_params=pltpu.CompilerParams(vmem_limit_bytes=12 << 20),
        cost_estimate=cost(queries, 1280),
        name="near",
    )(index, first, queries, keys, values, blocks)


def attend_far(index, first, queries, blocks, stats, sums, target_count):
    query_count = queries.shape[0]
    return pl.pallas_call(
        far_kernel,
        out_shape=jax.ShapeDtypeStruct((target_count, HEAD_SIZE, query_count), jnp.bfloat16),
        in_specs=[SMEM] + [VMEM] * 5,
        out_specs=VMEM,
        compiler_params=pltpu.CompilerParams(vmem_limit_bytes=12 << 20),
        cost_estimate=cost(queries, 1024),
        name="far",
    )(index, first, queries, blocks, stats, sums)


def exchange(x, axis, groups=None):
    return lax.all_to_all(x, axis, 0, 0, tiled=True, axis_index_groups=groups)


def per_device(queries, keys, values, doc_ids, out_weight):
    key_index, tok_index = (lax.axis_index(name) for name in ("key", "tok"))
    key_count, tok_count, kv_count = (lax.axis_size(name) for name in ("key", "tok", "kv"))
    row_count = queries.shape[0]
    slice_rows = row_count // tok_count
    index = jnp.stack([key_index, tok_index])
    pair = jnp.concatenate(
        [
            lax.dynamic_slice_in_dim(keys, tok_index * slice_rows, slice_rows, 0),
            lax.dynamic_slice_in_dim(values, tok_index * slice_rows, slice_rows, 0),
        ],
        axis=1,
    )
    like = [[place * PAIR + parity for place in range(key_count // PAIR)] for parity in range(PAIR)]
    copies = jnp.broadcast_to(pair[None], (key_count // PAIR,) + pair.shape)
    ranges = exchange(copies, "key", like)
    first = find_first(index, doc_ids.reshape(-1, LANES), row_count)
    chips = tok_count // CORES
    beside = [
        [(begin + parity) * tok_count + chip * CORES + core for parity in range(PAIR) for chip in range(chips)]
        for begin in range(0, key_count, PAIR)
        for core in range(CORES)
    ]
    blocks = exchange(pick(index, ranges, PAIR * chips), ("key", "tok"), beside)
    other_blocks = lax.ppermute(blocks, "tok", [(i, i ^ 1) for i in range(tok_count)])
    stats, sums = attend_near(index, first, queries, keys, values, blocks)
    attn = attend_far(index, first, queries, other_blocks, stats, sums, tok_count)
    attn = exchange(attn, "tok").reshape(tok_count * HEAD_SIZE, row_count)
    total = jnp.einsum("kq,kn->qn", attn, out_weight, preferred_element_type=jnp.float32)
    total = total.astype(jnp.bfloat16).reshape(kv_count, row_count // kv_count, -1)
    shares = exchange(total, "kv")
    return jnp.sum(shares.astype(jnp.float32), axis=0).astype(jnp.bfloat16)


def solution(mesh):
    placed = (P("key", ("kv", "tok")), P("key", "kv"), P("key", "kv"), P(), P("kv", "tok"))

    return jax.shard_map(per_device, mesh=mesh, in_specs=placed, out_specs=P(("key", "kv"), "tok"), check_vma=False)
```

profile of v0, /device:TPU:2, one launch (start us, length us, event | category | flops | bytes accessed | tf_op | source)
XLA Modules:
  0.0 92.7 jit_solution(16068943814549206542)
XLA Ops:
  0.0 0.0 copy-start
  0.0 0.0 copy-start.2
  0.0 0.0 copy-start.3
  0.0 0.0 copy-start.4
  0.0 0.0 copy-start.1
  0.0 0.9 constant_dynamic-slice_fusion
  0.9 0.7 broadcast_in_dim.2
  1.6 18.7 %all-to-all-start = ((bf16[8,32,256]{2,1,0:T(8,128)(2,1)}), bf16[8,32,256]{2,1,0:T(8,128)(2,1)S(1)}, u32[]{:S(2)}, u32[]{:S(2)}) async-start(bf16[8,32,256]{2,1,0:T(8,128)(2,1)} %broadcast_in_dim.2), calls=%async_computation | async-start | bytes 262144 | tf_op jit(solution)/shard_map/all_to_all | solution.py:177
  20.3 0.1 pad_add_fusion.index_ref
  20.4 16.4 %all-to-all-done.ranges_ref = bf16[8,32,256]{2,1,0:T(8,128)(2,1)S(1)} async-done(((bf16[8,32,256]{2,1,0:T(8,128)(2,1)}), bf16[8,32,256]{2,1,0:T(8,128)(2,1)S(1)}, u32[]{:S(2)}, u32[]{:S(2)}) %all-to-all-start) | async-done | bytes 131104 | tf_op jit(solution)/shard_map/all_to_all | solution.py:177
  36.8 0.6 pick.1
  37.4 11.4 %all_to_all.20.blocks_ref = bf16[8,4,32,256]{3,2,1,0:T(8,128)(2,1)S(1)} all-to-all(bf16[8,4,32,256]{3,2,1,0:T(8,128)(2,1)S(1)} %pick.1), channel_id=1, replica_groups={{0,2,4,6,8,10,12,14},{1,3,5,7,9,11,13,15},{16,18,20,22,24,26,28,30},{17..., dimensions={0} | all-to-all | bytes 1048576 | tf_op jit(solution)/shard_map/all_to_all | solution.py:177
  48.9 1.9 %collective-permute-start = (bf16[8,4,32,256]{3,2,1,0:T(8,128)(2,1)S(1)}, bf16[8,4,32,256]{3,2,1,0:T(8,128)(2,1)S(1)}, u32[]{:S(2)}, u32[]{:S(2)}) collective-permute-start(bf16[8,4,32,256]{3,2,1,0:T(8,128)(2,1)S(1)} %all_to_all.20.blocks_ref), channel_id=1, source_target_pairs={{0,1},{1,0},{2,3},{3,2},{4,5},{5,4},{6,7},{7,6},{8,9},{9,8},{10,11... | collective-permute-start | bytes 1572872 | tf_op jit(solution)/shard_map/ppermute | solution.py:204
  50.8 0.0 copy-done.4
  50.8 0.6 first.1.first_ref
  51.4 0.0 copy-done.2
  51.4 0.0 copy-done.3
  51.4 0.0 copy-done.1
  51.5 1.4 %near.1 = (f32[8,256]{1,0:T(8,128)S(1)}, f32[128,256]{1,0:T(8,128)S(1)}) custom-call(s32[2]{0:T(128)S(1)} %pad_add_fusion.index_ref, f32[1,256]{1,0:T(1,128)S(1)} %first.1.first_ref, bf16[256,128]{1,0:T(8,128)(2,1)S(1)} %copy-done.1, bf16[256,128]{1,0:T(8,128)(2,1)S(1)} %copy-done.3, bf16[256,128]{1,0:T(8,128)(2,1)S(1)} %copy-done.2, ...), custom_call_target="tpu_custom_call" | custom-call | flops 167772160 | bytes 1048576 | tf_op jit(solution)/shard_map/near/pallas_call | solution.py:149
  52.9 0.0 collective-permute-done.blocks_ref
  52.9 1.3 %far.1 = bf16[8,128,256]{2,1,0:T(8,128)(2,1)S(1)} custom-call(s32[2]{0:T(128)S(1)} %pad_add_fusion.index_ref, f32[1,256]{1,0:T(1,128)S(1)} %first.1.first_ref, bf16[256,128]{1,0:T(8,128)(2,1)S(1)} %copy-done.1, bf16[8,4,32,256]{3,2,1,0:T(8,128)(2,1)S(1)} %collective-permute-done.blocks_ref, f32[8,256]{1,0:T(8,128)S(1)} %get-tuple-element.7.stats_ref, ...), custom_call_target="tpu_custom_call" | custom-call | flops 134217728 | bytes 1048576 | tf_op jit(solution)/shard_map/far/pallas_call | solution.py:165
  54.1 13.1 %all_to_all.21 = bf16[8,128,256]{2,1,0:T(8,128)(2,1)S(1)} all-to-all(bf16[8,128,256]{2,1,0:T(8,128)(2,1)S(1)} %far.1), channel_id=1, replica_groups=mesh['kv'=8,'key'=16,'tok'=8] {'tok'}, dimensions={0} | all-to-all | bytes 1048576 | tf_op jit(solution)/shard_map/all_to_all | solution.py:177
  67.3 0.0 copy-done
  67.3 0.7 convolution_convert_fusion
  68.0 24.0 %all_to_all.22 = bf16[8,32,1024]{2,1,0:T(8,128)(2,1)S(1)} all-to-all(bf16[8,32,1024]{2,1,0:T(8,128)(2,1)S(1)} %bitcast.9), channel_id=1, replica_groups=mesh['kv'=8,'key'=16,'tok'=8] {'kv'}, dimensions={0} | all-to-all | bytes 1048576 | tf_op jit(solution)/shard_map/all_to_all | solution.py:177
  92.0 0.7 reduce_sum.12
  (1 shorter events, 0.0 us)
Async XLA Ops:
  0.0 67.3 %copy-start = (bf16[1024,1024]{1,0:T(8,128)(2,1)S(1)}, bf16[1024,1024]{1,0:T(8,128)(2,1)}, u32[]{:S(2)}) copy-start(bf16[1024,1024]{1,0:T(8,128)(2,1)} %param.9) | copy-start | bytes 6291460
  0.0 51.4 %copy-start.2 = (bf16[256,128]{1,0:T(8,128)(2,1)S(1)}, bf16[256,128]{1,0:T(8,128)(2,1)}, u32[]{:S(2)}) copy-start(bf16[256,128]{1,0:T(8,128)(2,1)} %values_ref.1) | copy-start | bytes 196612
  0.0 51.4 %copy-start.3 = (bf16[256,128]{1,0:T(8,128)(2,1)S(1)}, bf16[256,128]{1,0:T(8,128)(2,1)}, u32[]{:S(2)}) copy-start(bf16[256,128]{1,0:T(8,128)(2,1)} %keys_ref.1) | copy-start | bytes 196612
  0.0 50.8 %copy-start.4 = (s32[4096]{0:T(1024)S(1)}, s32[4096]{0:T(1024)}, u32[]{:S(2)}) copy-start(s32[4096]{0:T(1024)} %param.8) | copy-start | bytes 49156
  0.0 51.4 %copy-start.1 = (bf16[256,128]{1,0:T(8,128)(2,1)S(1)}, bf16[256,128]{1,0:T(8,128)(2,1)}, u32[]{:S(2)}) copy-start(bf16[256,128]{1,0:T(8,128)(2,1)} %queries_ref.3) | copy-start | bytes 196612
  1.6 35.2 %all-to-all-start = ((bf16[8,32,256]{2,1,0:T(8,128)(2,1)}), bf16[8,32,256]{2,1,0:T(8,128)(2,1)S(1)}, u32[]{:S(2)}, u32[]{:S(2)}) async-start(bf16[8,32,256]{2,1,0:T(8,128)(2,1)} %broadcast_in_dim.2), calls=%async_computation | async-start | bytes 262144 | tf_op jit(solution)/shard_map/all_to_all | solution.py:177
  48.9 4.0 %collective-permute-start = (bf16[8,4,32,256]{3,2,1,0:T(8,128)(2,1)S(1)}, bf16[8,4,32,256]{3,2,1,0:T(8,128)(2,1)S(1)}, u32[]{:S(2)}, u32[]{:S(2)}) collective-permute-start(bf16[8,4,32,256]{3,2,1,0:T(8,128)(2,1)S(1)} %all_to_all.20.blocks_ref), channel_id=1, source_target_pairs={{0,1},{1,0},{2,3},{3,2},{4,5},{5,4},{6,7},{7,6},{8,9},{9,8},{10,11... | collective-permute-start | bytes 1572872 | tf_op jit(solution)/shard_map/ppermute | solution.py:204
where the time goes:
time: 93.2 us; the launch traced here: 92.7 us
  blocking collectives  48.6 us (52%)
  starting transfers between devices  20.7 us (22%)
  waiting for transfers between devices  16.4 us (18%)
  Pallas kernels  3.89 us (4%)
  local copies, waits for them, and re-layouts  1.55 us (2%)
    all_to_all x3, blocking collectives, exchange(): return lax.all_to_all(x, axis, 0, 0, tiled=True, axis_index_groups=groups)  48.6 us
    all_to_all x1, starting transfers between devices, exchange(): return lax.all_to_all(x, axis, 0, 0, tiled=True, axis_index_groups=groups)  18.7 us
    all_to_all x1, waiting for transfers between devices, exchange(): return lax.all_to_all(x, axis, 0, 0, tiled=True, axis_index_groups=groups)  16.4 us
    ppermute x1, starting transfers between devices, per_device(): lax.ppermute(blocks, 'tok', [(i, i ^ 1) for i in range(tok_count)])  1.91 us
  transfers between devices with their start and end apart: 2, of which 1 were waited for; matrix products, arithmetic and copies ran while one was open for 0% of the time, Pallas kernels for 2%

commit v1 on v0

--- a/solution.py
+++ b/solution.py
@@ -19,18 +19,37 @@
 FACTOR = math.log2(math.e) / math.sqrt(HEAD_SIZE)
 
 VMEM = pl.BlockSpec(memory_space=pltpu.VMEM)
-SMEM = pl.BlockSpec(memory_space=pltpu.SMEM)
 
 
 def dot(a, b, contract):
     return lax.dot_general(a, b, (contract, ((), ())), preferred_element_type=jnp.float32)
 
 
-def first_kernel(index_ref, docs_ref, first_ref):
+def start_kernel(keys_ref, values_ref, docs_ref, out_ref, first_ref, pair_buf, docs_buf, sems):
+    copy_count, rows, _ = out_ref.shape
     query_count = first_ref.shape[1]
-    docs = docs_ref[...]
-    place = lax.broadcasted_iota(jnp.int32, (1, query_count), 1) + index_ref[0] * query_count
-    place = place.astype(jnp.float32)
+    begin = pl.multiple_of(lax.axis_index("tok") * rows, rows)
+    copies = [
+        pltpu.make_async_copy(
+            keys_ref.at[pl.ds(begin, rows), :], pair_buf.at[:, pl.ds(0, HEAD_SIZE)], sems.at[0]
+        ),
+        pltpu.make_async_copy(
+            values_ref.at[pl.ds(begin, rows), :],
+            pair_buf.at[:, pl.ds(HEAD_SIZE, HEAD_SIZE)],
+            sems.at[1],
+        ),
+        pltpu.make_async_copy(docs_ref, docs_buf, sems.at[2]),
+    ]
+    for copy in copies:
+        copy.start()
+    for copy in copies:
+        copy.wait()
+    pair = pair_buf[...]
+    for target in range(copy_count):
+        out_ref[target] = pair
+    docs = docs_buf[...]
+    place = lax.broadcasted_iota(jnp.int32, (1, query_count), 1)
+    place = (place + lax.axis_index("key") * query_count).astype(jnp.float32)
     first = jnp.zeros((1, query_count), jnp.float32)
     for number in range(1, MOST_DOC + 1):
         smaller = jnp.where(docs < number, 1.0, 0.0)
@@ -39,23 +58,33 @@
     first_ref[...] = first
 
 
-def find_first(index, docs, query_count):
-    return pl.pallas_call(
-        first_kernel,
-        out_shape=jax.ShapeDtypeStruct((1, query_count), jnp.float32),
-        in_specs=[SMEM, VMEM],
-        out_specs=VMEM,
+def start(keys, values, docs, copy_count, rows):
+    query_count = keys.shape[0]
+    hbm = pl.BlockSpec(memory_space=pltpu.HBM)
+    return pl.pallas_call(
+        start_kernel,
+        out_shape=[
+            jax.ShapeDtypeStruct((copy_count, rows, 2 * HEAD_SIZE), jnp.bfloat16),
+            jax.ShapeDtypeStruct((1, query_count), jnp.float32),
+        ],
+        in_specs=[hbm, hbm, hbm],
+        out_specs=[VMEM, VMEM],
+        scratch_shapes=[
+            pltpu.VMEM((rows, 2 * HEAD_SIZE), jnp.bfloat16),
+            pltpu.VMEM(docs.shape, jnp.int32),
+            pltpu.SemaphoreType.DMA((3,)),
+        ],
         compiler_params=pltpu.CompilerParams(vmem_limit_bytes=4 << 20),
-        name="first",
-    )(index, docs)
+        name="start",
+    )(*(pltpu.with_memory_space_constraint(x, pltpu.HBM) for x in (keys, values, docs)))
 
 
 def earliest(own, source_parity, taker_parity):
     return own // PAIR - NEEDED + taker_parity * (1 - source_parity)
 
 
-def pick_kernel(index_ref, ranges_ref, out_ref):
-    own = index_ref[0]
+def pick_kernel(ranges_ref, out_ref):
+    own = lax.axis_index("key")
     count = ranges_ref.shape[0]
     takers = out_ref.shape[0] // PAIR
     for parity in range(PAIR):
@@ -66,15 +95,15 @@
                 out_ref[parity * takers + taker, place] = block
 
 
-def pick(index, ranges, taker_count):
+def pick(ranges, taker_count):
     return pl.pallas_call(
         pick_kernel,
         out_shape=jax.ShapeDtypeStruct((taker_count, NEEDED) + ranges.shape[1:], jnp.bfloat16),
-        in_specs=[SMEM, VMEM],
+        in_specs=[VMEM],
         out_specs=VMEM,
         compiler_params=pltpu.CompilerParams(vmem_limit_bytes=8 << 20),
         name="pick",
-    )(index, ranges)
+    )(ranges)
 
 
 def mask_half(scores, own, core, first, blocks_shape, query_count):
@@ -95,9 +124,9 @@
 
 
 def near_kernel(
-    index_ref, first_ref, queries_ref, keys_ref, values_ref, blocks_ref, stats_ref, sums_ref
+    first_ref, queries_ref, keys_ref, values_ref, blocks_ref, stats_ref, sums_ref
 ):
-    own, core = index_ref[0], lax.rem(index_ref[1], CORES)
+    own, core = lax.axis_index("key"), lax.rem(lax.axis_index("tok"), CORES)
     query_count = queries_ref.shape[0]
     first = first_ref[...]
     blocks = blocks_ref[...].reshape(-1, 2 * HEAD_SIZE)
@@ -119,8 +148,8 @@
     sums_ref[...] = dot(values, weights.astype(jnp.bfloat16), ((0,), (0,)))
 
 
-def far_kernel(index_ref, first_ref, queries_ref, blocks_ref, stats_ref, sums_ref, out_ref):
-    own, core = index_ref[0], lax.rem(index_ref[1], CORES)
+def far_kernel(first_ref, queries_ref, blocks_ref, stats_ref, sums_ref, out_ref):
+    own, core = lax.axis_index("key"), lax.rem(lax.axis_index("tok"), CORES)
     query_count = queries_ref.shape[0]
     blocks = blocks_ref[...].reshape(-1, 2 * HEAD_SIZE)
     scores = dot(blocks[:, :HEAD_SIZE], queries_ref[...], ((1,), (1,)))
@@ -144,7 +173,7 @@
     )
 
 
-def attend_near(index, first, queries, keys, values, blocks):
+def attend_near(first, queries, keys, values, blocks):
     query_count = queries.shape[0]
     return pl.pallas_call(
         near_kernel,
@@ -152,25 +181,25 @@
             jax.ShapeDtypeStruct((8, query_count), jnp.float32),
             jax.ShapeDtypeStruct((HEAD_SIZE, query_count), jnp.float32),
         ],
-        in_specs=[SMEM] + [VMEM] * 5,
+        in_specs=[VMEM] * 5,
         out_specs=[VMEM, VMEM],
         compiler_params=pltpu.CompilerParams(vmem_limit_bytes=12 << 20),
         cost_estimate=cost(queries, 1280),
         name="near",
-    )(index, first, queries, keys, values, blocks)
-
-
-def attend_far(index, first, queries, blocks, stats, sums, target_count):
+    )(first, queries, keys, values, blocks)
+
+
+def attend_far(first, queries, blocks, stats, sums, target_count):
     query_count = queries.shape[0]
     return pl.pallas_call(
         far_kernel,
         out_shape=jax.ShapeDtypeStruct((target_count, HEAD_SIZE, query_count), jnp.bfloat16),
-        in_specs=[SMEM] + [VMEM] * 5,
+        in_specs=[VMEM] * 5,
         out_specs=VMEM,
         compiler_params=pltpu.CompilerParams(vmem_limit_bytes=12 << 20),
         cost_estimate=cost(queries, 1024),
         name="far",
-    )(index, first, queries, blocks, stats, sums)
+    )(first, queries, blocks, stats, sums)
 
 
 def exchange(x, axis, groups=None):
@@ -178,32 +207,23 @@
 
 
 def per_device(queries, keys, values, doc_ids, out_weight):
-    key_index, tok_index = (lax.axis_index(name) for name in ("key", "tok"))
     key_count, tok_count, kv_count = (lax.axis_size(name) for name in ("key", "tok", "kv"))
     row_count = queries.shape[0]
-    slice_rows = row_count // tok_count
-    index = jnp.stack([key_index, tok_index])
-    pair = jnp.concatenate(
-        [
-            lax.dynamic_slice_in_dim(keys, tok_index * slice_rows, slice_rows, 0),
-            lax.dynamic_slice_in_dim(values, tok_index * slice_rows, slice_rows, 0),
-        ],
-        axis=1,
+    like = [[place * PAIR + parity for place in range(key_count // PAIR)] for parity in range(PAIR)]
+    copies, first = start(
+        keys, values, doc_ids.reshape(-1, LANES), key_count // PAIR, row_count // tok_count
     )
-    like = [[place * PAIR + parity for place in range(key_count // PAIR)] for parity in range(PAIR)]
-    copies = jnp.broadcast_to(pair[None], (key_count // PAIR,) + pair.shape)
     ranges = exchange(copies, "key", like)
-    first = find_first(index, doc_ids.reshape(-1, LANES), row_count)
     chips = tok_count // CORES
     beside = [
         [(begin + parity) * tok_count + chip * CORES + core for parity in range(PAIR) for chip in range(chips)]
         for begin in range(0, key_count, PAIR)
         for core in range(CORES)
     ]
-    blocks = exchange(pick(index, ranges, PAIR * chips), ("key", "tok"), beside)
+    blocks = exchange(pick(ranges, PAIR * chips), ("key", "tok"), beside)
     other_blocks = lax.ppermute(blocks, "tok", [(i, i ^ 1) for i in range(tok_count)])
-    stats, sums = attend_near(index, first, queries, keys, values, blocks)
-    attn = attend_far(index, first, queries, other_blocks, stats, sums, tok_count)
+    stats, sums = attend_near(first, queries, keys, values, blocks)
+    attn = attend_far(first, queries, other_blocks, stats, sums, tok_count)
     attn = exchange(attn, "tok").reshape(tok_count * HEAD_SIZE, row_count)
     total = jnp.einsum("kq,kn->qn", attn, out_weight, preferred_element_type=jnp.float32)
     total = total.astype(jnp.bfloat16).reshape(kv_count, row_count // kv_count, -1)

time: 93.2 us -> 91.1 us (0.977)
  blocking collectives: 48.6 us -> 83.6 us
  starting transfers between devices: 20.7 us -> 1.91 us
  waiting for transfers between devices: 16.4 us -> 0.98 us
  local copies, waits for them, and re-layouts: 1.55 us -> 0.02 us
  Pallas kernels: 3.89 us -> 2.66 us
    all_to_all x3 -> x4, blocking collectives: 48.6 us -> 83.6 us  [exchange(): return lax.all_to_all(x, axis, 0, 0, tiled=True, axis_index_groups=groups)]
    all_to_all x1 -> x0, starting transfers between devices: 18.7 us -> none  [exchange(): return lax.all_to_all(x, axis, 0, 0, tiled=True, axis_index_groups=groups)]
    all_to_all x1 -> x0, waiting for transfers between devices: 16.4 us -> none  [exchange(): return lax.all_to_all(x, axis, 0, 0, tiled=True, axis_index_groups=groups)]
    ppermute x1, waiting for transfers between devices: 0.01 us -> 0.98 us  [per_device(): lax.ppermute(blocks, 'tok', [(i, i ^ 1) for i in range(tok_count)])]
  transfers between devices with their start and end apart: 2 -> 1, of which waited for: 1 -> 1; matrix products, arithmetic and copies ran while one was open for 0% -> 0% of each run, Pallas kernels for 2% -> 1%
where the time goes in v1:
time: 91.1 us; the launch traced here: 90.7 us
  blocking collectives  83.6 us (92%)
  Pallas kernels  2.66 us (3%)
  starting transfers between devices  1.91 us (2%)
  waiting for transfers between devices  0.98 us (1%)
    all_to_all x4, blocking collectives, exchange(): return lax.all_to_all(x, axis, 0, 0, tiled=True, axis_index_groups=groups)  83.6 us
    ppermute x1, starting transfers between devices, per_device(): lax.ppermute(blocks, 'tok', [(i, i ^ 1) for i in range(tok_count)])  1.91 us
  transfers between devices with their start and end apart: 1, of which 1 were waited for; matrix products, arithmetic and copies ran while one was open for 0% of the time, Pallas kernels for 1%

profile of v1, /device:TPU:2, one launch (start us, length us, event | category | flops | bytes accessed | tf_op | source)
XLA Modules:
  0.0 90.7 jit_solution(9901546869545750352)
XLA Ops:
  0.0 0.0 copy-start
  0.0 0.0 copy-start.2
  0.0 0.0 copy-start.3
  0.0 0.0 copy-start.1
  0.0 1.0 %start.1 = (bf16[8,32,256]{2,1,0:T(8,128)(2,1)S(1)}, f32[1,256]{1,0:T(1,128)S(1)}) custom-call(bf16[256,128]{1,0:T(8,128)(2,1)} %keys_ref.3, bf16[256,128]{1,0:T(8,128)(2,1)} %values_ref.3, s32[32,128]{1,0:T(8,128)} %bitcast.7), custom_call_target="tpu_custom_call" | custom-call | tf_op jit(solution)/shard_map/start/pallas_call | solution.py:64
  1.1 35.0 %all_to_all.20.ranges_ref = bf16[8,32,256]{2,1,0:T(8,128)(2,1)S(1)} all-to-all(bf16[8,32,256]{2,1,0:T(8,128)(2,1)S(1)} %get-tuple-element.10), channel_id=1, replica_groups={{0,16,32,48,64,80,96,112},{8,24,40,56,72,88,104,120},{1,17,33,49,65,81,..., dimensions={0} | all-to-all | bytes 262144 | tf_op jit(solution)/shard_map/all_to_all | solution.py:206
  36.1 11.4 %all_to_all.21.blocks_ref = bf16[8,4,32,256]{3,2,1,0:T(8,128)(2,1)S(1)} all-to-all(bf16[8,4,32,256]{3,2,1,0:T(8,128)(2,1)S(1)} %pick.1), channel_id=1, replica_groups={{0,2,4,6,8,10,12,14},{1,3,5,7,9,11,13,15},{16,18,20,22,24,26,28,30},{17..., dimensions={0} | all-to-all | bytes 1048576 | tf_op jit(solution)/shard_map/all_to_all | solution.py:206
  47.6 1.9 %collective-permute-start = (bf16[8,4,32,256]{3,2,1,0:T(8,128)(2,1)S(1)}, bf16[8,4,32,256]{3,2,1,0:T(8,128)(2,1)S(1)}, u32[]{:S(2)}, u32[]{:S(2)}) collective-permute-start(bf16[8,4,32,256]{3,2,1,0:T(8,128)(2,1)S(1)} %all_to_all.21.blocks_ref), channel_id=1, source_target_pairs={{0,1},{1,0},{2,3},{3,2},{4,5},{5,4},{6,7},{7,6},{8,9},{9,8},{10,11... | collective-permute-start | bytes 1572872 | tf_op jit(solution)/shard_map/ppermute | solution.py:224
  49.5 0.0 copy-done.2
  49.5 0.0 copy-done.3
  49.5 0.0 copy-done.1
  49.5 0.9 near.1
  50.4 1.0 %collective-permute-done.blocks_ref = bf16[8,4,32,256]{3,2,1,0:T(8,128)(2,1)S(1)} collective-permute-done((bf16[8,4,32,256]{3,2,1,0:T(8,128)(2,1)S(1)}, bf16[8,4,32,256]{3,2,1,0:T(8,128)(2,1)S(1)}, u32[]{:S(2)}, u32[]{:S(2)}) %collective-permute-start) | collective-permute-done | bytes 524320 | tf_op jit(solution)/shard_map/ppermute | solution.py:224
  51.4 0.7 far.1
  52.1 13.1 %all_to_all.22 = bf16[8,128,256]{2,1,0:T(8,128)(2,1)S(1)} all-to-all(bf16[8,128,256]{2,1,0:T(8,128)(2,1)S(1)} %far.1), channel_id=1, replica_groups=mesh['kv'=8,'key'=16,'tok'=8] {'tok'}, dimensions={0} | all-to-all | bytes 1048576 | tf_op jit(solution)/shard_map/all_to_all | solution.py:206
  65.2 0.0 copy-done
  65.2 0.7 convolution_convert_fusion
  66.0 24.0 %all_to_all.23 = bf16[8,32,1024]{2,1,0:T(8,128)(2,1)S(1)} all-to-all(bf16[8,32,1024]{2,1,0:T(8,128)(2,1)S(1)} %bitcast.6), channel_id=1, replica_groups=mesh['kv'=8,'key'=16,'tok'=8] {'kv'}, dimensions={0} | all-to-all | bytes 1048576 | tf_op jit(solution)/shard_map/all_to_all | solution.py:206
  90.0 0.7 reduce_sum.12
  (1 shorter events, 0.0 us)
Async XLA Ops:
  0.0 65.2 %copy-start = (bf16[1024,1024]{1,0:T(8,128)(2,1)S(1)}, bf16[1024,1024]{1,0:T(8,128)(2,1)}, u32[]{:S(2)}) copy-start(bf16[1024,1024]{1,0:T(8,128)(2,1)} %param.9) | copy-start | bytes 6291460
  0.0 49.5 %copy-start.2 = (bf16[256,128]{1,0:T(8,128)(2,1)S(1)}, bf16[256,128]{1,0:T(8,128)(2,1)}, u32[]{:S(2)}) copy-start(bf16[256,128]{1,0:T(8,128)(2,1)} %keys_ref.3) | copy-start | bytes 196612
  0.0 49.5 %copy-start.3 = (bf16[256,128]{1,0:T(8,128)(2,1)S(1)}, bf16[256,128]{1,0:T(8,128)(2,1)}, u32[]{:S(2)}) copy-start(bf16[256,128]{1,0:T(8,128)(2,1)} %values_ref.3) | copy-start | bytes 196612
  0.0 49.5 %copy-start.1 = (bf16[256,128]{1,0:T(8,128)(2,1)S(1)}, bf16[256,128]{1,0:T(8,128)(2,1)}, u32[]{:S(2)}) copy-start(bf16[256,128]{1,0:T(8,128)(2,1)} %queries_ref.3) | copy-start | bytes 196612
  47.6 3.8 %collective-permute-start = (bf16[8,4,32,256]{3,2,1,0:T(8,128)(2,1)S(1)}, bf16[8,4,32,256]{3,2,1,0:T(8,128)(2,1)S(1)}, u32[]{:S(2)}, u32[]{:S(2)}) collective-permute-start(bf16[8,4,32,256]{3,2,1,0:T(8,128)(2,1)S(1)} %all_to_all.21.blocks_ref), channel_id=1, source_target_pairs={{0,1},{1,0},{2,3},{3,2},{4,5},{5,4},{6,7},{7,6},{8,9},{9,8},{10,11... | collective-permute-start | bytes 1572872 | tf_op jit(solution)/shard_map/ppermute | solution.py:224

commit v2 on v1

v2 whole, which is shorter than its diff:
```python
import math

import jax
import jax.numpy as jnp
from jax import lax
from jax.experimental import pallas as pl
from jax.experimental.pallas import tpu as pltpu
from jax.sharding import PartitionSpec as P


HEAD_SIZE = 128
REACH = 8
LOW = -1e30
MOST_DOC = 5
LANES = 128
CORES = 2
PAIR = 2
FACTOR = math.log2(math.e) / math.sqrt(HEAD_SIZE)

VMEM = pl.BlockSpec(memory_space=pltpu.VMEM)


def dot(a, b, contract):
    return lax.dot_general(a, b, (contract, ((), ())), preferred_element_type=jnp.float32)


def start_kernel(
    queries_ref, keys_ref, values_ref, docs_ref, out_ref, first_ref, own_ref, docs_buf, sems
):
    rows = out_ref.shape[0]
    query_count = first_ref.shape[1]
    begin = pl.multiple_of(lax.rem(lax.axis_index("tok"), CORES) * rows, rows)
    copies = [pltpu.make_async_copy(docs_ref, docs_buf, sems.at[0])]
    for place, source in enumerate((keys_ref, values_ref, queries_ref)):
        copies.append(pltpu.make_async_copy(source, own_ref.at[place], sems.at[place + 1]))
    for copy in copies:
        copy.start()
    for copy in copies:
        copy.wait()
    out_ref[:, :HEAD_SIZE] = own_ref[0, pl.ds(begin, rows), :]
    out_ref[:, HEAD_SIZE:] = own_ref[1, pl.ds(begin, rows), :]
    docs = docs_buf[...]
    place = lax.broadcasted_iota(jnp.int32, (1, query_count), 1)
    place = (place + lax.axis_index("key") * query_count).astype(jnp.float32)
    first = jnp.zeros((1, query_count), jnp.float32)
    for number in range(1, MOST_DOC + 1):
        smaller = jnp.where(docs < number, 1.0, 0.0)
        begins = jnp.sum(jnp.sum(smaller, axis=0, keepdims=True), axis=1, keepdims=True)
        first = jnp.where(begins <= place, jnp.maximum(first, begins), first)
    first_ref[...] = first


def start(queries, keys, values, docs):
    query_count = keys.shape[0]
    hbm = pl.BlockSpec(memory_space=pltpu.HBM)
    return pl.pallas_call(
        start_kernel,
        out_shape=[
            jax.ShapeDtypeStruct((query_count // CORES, 2 * HEAD_SIZE), jnp.bfloat16),
            jax.ShapeDtypeStruct((1, query_count), jnp.float32),
            jax.ShapeDtypeStruct((3,) + keys.shape, jnp.bfloat16),
        ],
        in_specs=[hbm] * 4,
        out_specs=[VMEM] * 3,
        scratch_shapes=[
            pltpu.VMEM(docs.shape, jnp.int32),
            pltpu.SemaphoreType.DMA((4,)),
        ],
        compiler_params=pltpu.CompilerParams(vmem_limit_bytes=4 << 20),
        name="start",
    )(*(pltpu.with_memory_space_constraint(x, pltpu.HBM) for x in (queries, keys, values, docs)))


def shift_of(chip, core):
    return jnp.where(core == 0, REACH - PAIR * chip, PAIR + PAIR * chip)


def pick_kernel(half_ref, held_ref, out_ref):
    own, tok = lax.axis_index("key"), lax.axis_index("tok")
    takers = out_ref.shape[0] // PAIR
    held = held_ref[...]
    swapped = (lax.rem(own, PAIR) == 0) & (shift_of(tok // CORES, lax.rem(tok, CORES)) == REACH)
    for taker in range(takers):
        out_ref[taker] = held
    beside = jnp.where(swapped, half_ref[...].astype(jnp.float32), held.astype(jnp.float32))
    beside = beside.astype(jnp.bfloat16)
    for taker in range(takers):
        out_ref[takers + taker] = beside


def pick(half, held, taker_count):
    return pl.pallas_call(
        pick_kernel,
        out_shape=jax.ShapeDtypeStruct((taker_count,) + held.shape, jnp.bfloat16),
        in_specs=[VMEM, VMEM],
        out_specs=VMEM,
        compiler_params=pltpu.CompilerParams(vmem_limit_bytes=8 << 20),
        name="pick",
    )(half, held)


def mask_half(scores, own, core, first, blocks_shape, query_count):
    source_count, rows, _ = blocks_shape
    row = lax.broadcasted_iota(jnp.int32, (rows, query_count), 0).astype(jnp.float32)
    chips = source_count // PAIR
    pieces = []
    for source in range(source_count):
        parity, chip = source // chips, source % chips
        shift = shift_of(chip, core)
        if parity == 0:
            shift = jnp.where((lax.rem(own, PAIR) == 1) & (shift == REACH), 0, shift)
        number = own // PAIR * PAIR + parity - shift
        start = number * query_count + core * rows
        allowed = row >= first - start.astype(jnp.float32)
        pieces.append(jnp.where(allowed, scores[source * rows : (source + 1) * rows] * FACTOR, LOW))
    return pieces


def near_kernel(first_ref, own_ref, blocks_ref, stats_ref, sums_ref):
    own, core = lax.axis_index("key"), lax.rem(lax.axis_index("tok"), CORES)
    query_count = first_ref.shape[1]
    first = first_ref[...]
    blocks = blocks_ref[...].reshape(-1, 2 * HEAD_SIZE)
    queries = own_ref[2]
    scores = dot(blocks[:, :HEAD_SIZE], queries, ((1,), (1,)))
    pieces = mask_half(scores, own, core, first, blocks_ref.shape, query_count)
    scores = dot(own_ref[0], queries, ((1,), (1,)))
    row = lax.broadcasted_iota(jnp.int32, scores.shape, 0)
    lane = lax.broadcasted_iota(jnp.int32, scores.shape, 1)
    begin = first - (own * query_count).astype(jnp.float32)
    allowed = (row <= lane) & (row.astype(jnp.float32) >= begin)
    pieces.append(jnp.where(allowed, scores * FACTOR, LOW))
    scores = jnp.concatenate(pieces, axis=0)
    highest = jnp.max(scores, axis=0, keepdims=True)
    weights = jnp.exp2(scores - highest)
    stats_ref[0:1, :] = highest
    stats_ref[1:2, :] = jnp.sum(weights, axis=0, keepdims=True)
    values = jnp.concatenate([blocks[:, HEAD_SIZE:], own_ref[1]], axis=0)
    sums_ref[...] = dot(values, weights.astype(jnp.bfloat16), ((0,), (0,)))


def far_kernel(first_ref, own_ref, blocks_ref, stats_ref, sums_ref, out_ref):
    own, core = lax.axis_index("key"), lax.rem(lax.axis_index("tok"), CORES)
    query_count = first_ref.shape[1]
    blocks = blocks_ref[...].reshape(-1, 2 * HEAD_SIZE)
    scores = dot(blocks[:, :HEAD_SIZE], own_ref[2], ((1,), (1,)))
    pieces = mask_half(scores, own, 1 - core, first_ref[...], blocks_ref.shape, query_count)
    scores = jnp.concatenate(pieces, axis=0)
    before = stats_ref[0:1, :]
    highest = jnp.maximum(before, jnp.max(scores, axis=0, keepdims=True))
    weights = jnp.exp2(scores - highest)
    keep = jnp.exp2(before - highest)
    total = keep * stats_ref[1:2, :] + jnp.sum(weights, axis=0, keepdims=True)
    weighted = dot(blocks[:, HEAD_SIZE:], weights.astype(jnp.bfloat16), ((0,), (0,)))
    attn = ((keep * sums_ref[...] + weighted) * (1.0 / total)).astype(jnp.bfloat16)
    for target in range(out_ref.shape[0]):
        out_ref[target] = attn


def cost(query_count, key_count):
    scores = query_count * key_count
    return pl.CostEstimate(
        flops=4 * HEAD_SIZE * scores, transcendentals=scores, bytes_accessed=1 << 20
    )


def attend_near(first, own, blocks):
    query_count = first.shape[1]
    return pl.pallas_call(
        near_kernel,
        out_shape=[
            jax.ShapeDtypeStruct((8, query_count), jnp.float32),
            jax.ShapeDtypeStruct((HEAD_SIZE, query_count), jnp.float32),
        ],
        in_specs=[VMEM] * 3,
        out_specs=[VMEM, VMEM],
        compiler_params=pltpu.CompilerParams(vmem_limit_bytes=12 << 20),
        cost_estimate=cost(query_count, blocks.shape[0] * blocks.shape[1] + query_count),
        name="near",
    )(first, own, blocks)


def attend_far(first, own, blocks, stats, sums, target_count):
    query_count = first.shape[1]
    return pl.pallas_call(
        far_kernel,
        out_shape=jax.ShapeDtypeStruct((target_count, HEAD_SIZE, query_count), jnp.bfloat16),
        in_specs=[VMEM] * 5,
        out_specs=VMEM,
        compiler_params=pltpu.CompilerParams(vmem_limit_bytes=12 << 20),
        cost_estimate=cost(query_count, blocks.shape[0] * blocks.shape[1]),
        name="far",
    )(first, own, blocks, stats, sums)


def exchange(x, axis, groups=None):
    return lax.all_to_all(x, axis, 0, 0, tiled=True, axis_index_groups=groups)


def per_device(queries, keys, values, doc_ids, out_weight):
    key_count, tok_count, kv_count = (lax.axis_size(name) for name in ("key", "tok", "kv"))
    row_count = queries.shape[0]
    half, first, own = start(queries, keys, values, doc_ids.reshape(-1, LANES))
    chips = tok_count // CORES
    beside = [
        [(begin + parity) * tok_count + chip * CORES + core for parity in range(PAIR) for chip in range(chips)]
        for begin in range(0, key_count, PAIR)
        for core in range(CORES)
    ]
    shifts = [REACH - tok if tok % CORES == 0 else PAIR + tok - 1 for tok in range(tok_count)]
    later = [
        (begin * tok_count + tok, (begin + shifts[tok]) * tok_count + tok)
        for begin in range(key_count)
        for tok in range(tok_count)
        if begin + shifts[tok] < key_count
    ]
    held = lax.ppermute(half, ("key", "tok"), later)
    blocks = exchange(pick(half, held, PAIR * chips), ("key", "tok"), beside)
    other_blocks = lax.ppermute(blocks, "tok", [(i, i ^ 1) for i in range(tok_count)])
    stats, sums = attend_near(first, own, blocks)
    attn = attend_far(first, own, other_blocks, stats, sums, tok_count)
    attn = exchange(attn, "tok").reshape(tok_count * HEAD_SIZE, row_count)
    total = jnp.einsum("kq,kn->qn", attn, out_weight, preferred_element_type=jnp.float32)
    total = total.astype(jnp.bfloat16).reshape(kv_count, row_count // kv_count, -1)
    shares = exchange(total, "kv")
    return jnp.sum(shares.astype(jnp.float32), axis=0).astype(jnp.bfloat16)


def solution(mesh):
    placed = (P("key", ("kv", "tok")), P("key", "kv"), P("key", "kv"), P(), P("kv", "tok"))

    return jax.shard_map(per_device, mesh=mesh, in_specs=placed, out_specs=P(("key", "kv"), "tok"), check_vma=False)
```

time: 91.1 us -> 78.3 us (0.86)
  blocking collectives: 83.6 us -> 54.3 us
  starting transfers between devices: 1.91 us -> 16.5 us
  waiting for transfers between devices: 0.98 us -> 2.86 us
    all_to_all x4 -> x3, blocking collectives: 83.6 us -> 54.3 us  [exchange(): return lax.all_to_all(x, axis, 0, 0, tiled=True, axis_index_groups=groups)]
    ppermute x0 -> x1, starting transfers between devices: none -> 14.5 us  [per_device(): held = lax.ppermute(half, ('key', 'tok'), later)]
    ppermute x0 -> x1, waiting for transfers between devices: none -> 1.88 us  [per_device(): held = lax.ppermute(half, ('key', 'tok'), later)]
  transfers between devices with their start and end apart: 1 -> 2, of which waited for: 1 -> 2; matrix products, arithmetic and copies ran while one was open for 0% -> 0% of each run, Pallas kernels for 1% -> 1%
where the time goes in v2:
time: 78.3 us; the launch traced here: 78 us
  blocking collectives  54.3 us (69%)
  starting transfers between devices  16.5 us (21%)
  waiting for transfers between devices  2.86 us (4%)
  Pallas kernels  2.83 us (4%)
    all_to_all x3, blocking collectives, exchange(): return lax.all_to_all(x, axis, 0, 0, tiled=True, axis_index_groups=groups)  54.3 us
    ppermute x1, starting transfers between devices, per_device(): held = lax.ppermute(half, ('key', 'tok'), later)  14.5 us
    ppermute x1, starting transfers between devices, per_device(): lax.ppermute(blocks, 'tok', [(i, i ^ 1) for i in range(tok_count)])  1.94 us
    ppermute x1, waiting for transfers between devices, per_device(): held = lax.ppermute(half, ('key', 'tok'), later)  1.88 us
  transfers between devices with their start and end apart: 2, of which 2 were waited for; matrix products, arithmetic and copies ran while one was open for 0% of the time, Pallas kernels for 1%

profile of v2, /device:TPU:2, one launch (start us, length us, event | category | flops | bytes accessed | tf_op | source)
XLA Modules:
  0.0 78.0 jit_solution(13007110517347870188)
XLA Ops:
  0.0 0.0 copy-start
  0.0 1.2 %start.1 = (bf16[128,256]{1,0:T(8,128)(2,1)S(1)}, f32[1,256]{1,0:T(1,128)S(1)}, bf16[3,256,128]{2,1,0:T(8,128)(2,1)S(1)}) custom-call(bf16[256,128]{1,0:T(8,128)(2,1)} %queries_ref.1, bf16[256,128]{1,0:T(8,128)(2,1)} %keys_ref.1, bf16[256,128]{1,0:T(8,128)(2,1)} %values_ref.1, s32[32,128]{1,0:T(8,128)} %bitcast.7), custom_call_target="tpu_custom_call" | custom-call | tf_op jit(solution)/shard_map/start/pallas_call | solution.py:56
  1.2 14.5 %collective-permute-start = (bf16[128,256]{1,0:T(8,128)(2,1)S(1)}, bf16[128,256]{1,0:T(8,128)(2,1)S(1)}, u32[]{:S(2)}, u32[]{:S(2)}) collective-permute-start(bf16[128,256]{1,0:T(8,128)(2,1)S(1)} %get-tuple-element.12.half_ref), channel_id=1, source_target_pairs={{0,64},{1,17},{2,50},{3,35},{4,36},{5,53},{6,22},{7,71},{8,72},{9,... | collective-permute-start | bytes 196616 | tf_op jit(solution)/shard_map/ppermute | solution.py:217
  15.8 1.9 %collective-permute-done.held_ref = bf16[128,256]{1,0:T(8,128)(2,1)S(1)} collective-permute-done((bf16[128,256]{1,0:T(8,128)(2,1)S(1)}, bf16[128,256]{1,0:T(8,128)(2,1)S(1)}, u32[]{:S(2)}, u32[]{:S(2)}) %collective-permute-start) | collective-permute-done | bytes 65568 | tf_op jit(solution)/shard_map/ppermute | solution.py:217
  17.7 17.3 %all_to_all.15.blocks_ref = bf16[8,128,256]{2,1,0:T(8,128)(2,1)S(1)} all-to-all(bf16[8,128,256]{2,1,0:T(8,128)(2,1)S(1)} %pick.1), channel_id=1, replica_groups={{0,2,4,6,8,10,12,14},{1,3,5,7,9,11,13,15},{16,18,20,22,24,26,28,30},{17..., dimensions={0} | all-to-all | bytes 1048576 | tf_op jit(solution)/shard_map/all_to_all | solution.py:197
  34.9 1.9 %collective-permute-start.1 = (bf16[8,128,256]{2,1,0:T(8,128)(2,1)S(1)}, bf16[8,128,256]{2,1,0:T(8,128)(2,1)S(1)}, u32[]{:S(2)}, u32[]{:S(2)}) collective-permute-start(bf16[8,128,256]{2,1,0:T(8,128)(2,1)S(1)} %all_to_all.15.blocks_ref), channel_id=1, source_target_pairs={{0,1},{1,0},{2,3},{3,2},{4,5},{5,4},{6,7},{7,6},{8,9},{9,8},{10,11... | collective-permute-start | bytes 1572872 | tf_op jit(solution)/shard_map/ppermute | solution.py:219
  36.9 0.9 %near.1 = (f32[8,256]{1,0:T(8,128)S(1)}, f32[128,256]{1,0:T(8,128)S(1)}) custom-call(f32[1,256]{1,0:T(1,128)S(1)} %get-tuple-element.10.first_ref, bf16[3,256,128]{2,1,0:T(8,128)(2,1)S(1)} %get-tuple-element.11.own_ref, bf16[8,128,256]{2,1,0:T(8,128)(2,1)S(1)} %all_to_all.15.blocks_ref), custom_call_target="tpu_custom_call" | custom-call | flops 167772160 | bytes 1048576 | tf_op jit(solution)/shard_map/near/pallas_call | solution.py:169
  37.8 1.0 %collective-permute-done.1.blocks_ref = bf16[8,128,256]{2,1,0:T(8,128)(2,1)S(1)} collective-permute-done((bf16[8,128,256]{2,1,0:T(8,128)(2,1)S(1)}, bf16[8,128,256]{2,1,0:T(8,128)(2,1)S(1)}, u32[]{:S(2)}, u32[]{:S(2)}) %collective-permute-start.1) | collective-permute-done | bytes 524320 | tf_op jit(solution)/shard_map/ppermute | solution.py:219
  38.7 0.7 far.1
  39.5 13.0 %all_to_all.16 = bf16[8,128,256]{2,1,0:T(8,128)(2,1)S(1)} all-to-all(bf16[8,128,256]{2,1,0:T(8,128)(2,1)S(1)} %far.1), channel_id=1, replica_groups=mesh['kv'=8,'key'=16,'tok'=8] {'tok'}, dimensions={0} | all-to-all | bytes 1048576 | tf_op jit(solution)/shard_map/all_to_all | solution.py:197
  52.5 0.0 copy-done
  52.5 0.7 convolution_convert_fusion
  53.2 24.0 %all_to_all.17 = bf16[8,32,1024]{2,1,0:T(8,128)(2,1)S(1)} all-to-all(bf16[8,32,1024]{2,1,0:T(8,128)(2,1)S(1)} %bitcast.6), channel_id=1, replica_groups=mesh['kv'=8,'key'=16,'tok'=8] {'kv'}, dimensions={0} | all-to-all | bytes 1048576 | tf_op jit(solution)/shard_map/all_to_all | solution.py:197
  77.3 0.7 reduce_sum.12
  (1 shorter events, 0.0 us)
Async XLA Ops:
  0.0 52.5 %copy-start = (bf16[1024,1024]{1,0:T(8,128)(2,1)S(1)}, bf16[1024,1024]{1,0:T(8,128)(2,1)}, u32[]{:S(2)}) copy-start(bf16[1024,1024]{1,0:T(8,128)(2,1)} %param.9) | copy-start | bytes 6291460
  1.2 16.4 %collective-permute-start = (bf16[128,256]{1,0:T(8,128)(2,1)S(1)}, bf16[128,256]{1,0:T(8,128)(2,1)S(1)}, u32[]{:S(2)}, u32[]{:S(2)}) collective-permute-start(bf16[128,256]{1,0:T(8,128)(2,1)S(1)} %get-tuple-element.12.half_ref), channel_id=1, source_target_pairs={{0,64},{1,17},{2,50},{3,35},{4,36},{5,53},{6,22},{7,71},{8,72},{9,... | collective-permute-start | bytes 196616 | tf_op jit(solution)/shard_map/ppermute | solution.py:217
  34.9 3.8 %collective-permute-start.1 = (bf16[8,128,256]{2,1,0:T(8,128)(2,1)S(1)}, bf16[8,128,256]{2,1,0:T(8,128)(2,1)S(1)}, u32[]{:S(2)}, u32[]{:S(2)}) collective-permute-start(bf16[8,128,256]{2,1,0:T(8,128)(2,1)S(1)} %all_to_all.15.blocks_ref), channel_id=1, source_target_pairs={{0,1},{1,0},{2,3},{3,2},{4,5},{5,4},{6,7},{7,6},{8,9},{9,8},{10,11... | collective-permute-start | bytes 1572872 | tf_op jit(solution)/shard_map/ppermute | solution.py:219
